TPU v7x, 512 devices: a whole 4x4x16 slice. The times are simulated.
512 devices in a mesh: section: 8 (over x_lo, y), seq: 64 (over x_hi, z, core).
Axes of the slice: x: 4 (x_hi: 2, x_lo: 2; x = x_hi * 2 + x_lo), y: 4, z: 16, core: 2. Of those that a mesh axis runs over, the one named last changes fastest.
Arguments:
- resident_microbatches: bfloat16 [8, 8192, 1024], P('section', 'seq'), may hold values from -64 to 64
- arriving_microbatch: bfloat16 [8192, 1024], P('seq'), may hold values from -64 to 64
- prenormal_scaling: float32 [8, 1024], P('section'), may hold values from 0.1 to 1.9
- attention_triple_matrix: bfloat16 [8, 1024, 3072], P('section', 'seq'), may hold values from -0.1875 to 0.1875
- exit_projection_matrix: bfloat16 [8, 1024, 1024], P('section'), may hold values from -0.1875 to 0.1875
- mirrored_lookup_tile: int32 [64, 4], replicated, may hold values from 0 to 1
Outputs:
- tick_out: bfloat16 [2, 8, 8192, 1024], P(None, 'section', 'seq')
All inputs are finite; a program needn't handle non-finite values.
Results may differ from a plain program's by a relative error of at most 0.004.
Values may be sent and summed in bfloat16 or wider, within the bound.
A program may use at most 64 MiB of HBM per device.

v0:
```python
import jax
import jax.numpy as jnp
from jax import lax
from jax.sharding import PartitionSpec as P

HEADS = 8
HEAD = 128
BLOCK = 64
LEVELS = 4
epsilon = 1e-06


def swapped(x, axis, stride):
    return lax.ppermute(x, axis, [(i, i ^ 1 << stride) for i in range(lax.axis_size(axis))])


def from_behind(block, axis, distance):
    devices = range(lax.axis_size(axis))
    route = [(i - distance, i) for i in devices if i - distance in devices]
    return lax.ppermute(block, axis, route)


def head_norm(projected, row_count):
    shaped = projected.reshape(row_count, HEADS, HEAD)
    mean_square = jnp.mean(shaped * shaped, axis=-1, keepdims=True)
    return (shaped * lax.rsqrt(mean_square + epsilon)).astype(jnp.bfloat16)


def transform_through_tier(
    hidden_in, gain_row, weights, out_weights, mirrored_lookup_tile, compute_unit
):
    row_count = hidden_in.shape[0]
    blocks = row_count // BLOCK
    inner_width = HEADS * HEAD
    widened = hidden_in.astype(jnp.float32)
    mean_square = jnp.mean(widened * widened, axis=-1, keepdims=True)
    normed = (widened * lax.rsqrt(mean_square + epsilon) * gain_row).astype(jnp.bfloat16)
    projected = jnp.dot(normed, weights, preferred_element_type=jnp.float32)
    queries = head_norm(projected[:, :inner_width], row_count)
    key_rows = head_norm(projected[:, inner_width : 2 * inner_width], row_count).reshape(
        row_count, inner_width
    )
    values = projected[:, 2 * inner_width :].astype(jnp.bfloat16)
    key_value = jnp.stack([key_rows, values])
    remote = []
    for bit_level in range(LEVELS):
        arrived = swapped(key_value, "seq", bit_level)
        wanted = mirrored_lookup_tile[compute_unit, bit_level]
        remote.append(lax.dynamic_slice_in_dim(arrived, wanted * BLOCK, BLOCK, 1))
    remote = jnp.concatenate(remote, axis=1)
    far_keys = jnp.broadcast_to(
        remote[0].reshape(1, LEVELS * BLOCK, HEADS, HEAD), (blocks, LEVELS * BLOCK, HEADS, HEAD)
    )
    far_values = jnp.broadcast_to(
        remote[1].reshape(1, LEVELS * BLOCK, HEADS, HEAD), (blocks, LEVELS * BLOCK, HEADS, HEAD)
    )
    query_blocks = queries.reshape(blocks, BLOCK, HEADS, HEAD)
    all_keys = jnp.concatenate([key_rows.reshape(blocks, BLOCK, HEADS, HEAD), far_keys], axis=1)
    all_values = jnp.concatenate([values.reshape(blocks, BLOCK, HEADS, HEAD), far_values], axis=1)
    score_scale = HEAD ** (-0.5)
    scores = (
        jnp.einsum("cqhd,ckhd->chqk", query_blocks, all_keys, preferred_element_type=jnp.float32)
        * score_scale
    )
    exps = jnp.exp(scores)
    weights_soft = (exps / jnp.sum(exps, axis=-1, keepdims=True)).astype(jnp.bfloat16)
    mixed_heads = jnp.einsum(
        "chqk,ckhd->cqhd", weights_soft, all_values, preferred_element_type=jnp.float32
    )
    attended = mixed_heads.astype(jnp.bfloat16).reshape(row_count, inner_width)
    return (widened + jnp.dot(attended, out_weights, preferred_element_type=jnp.float32)).astype(
        jnp.bfloat16
    )


def per_device(
    resident_microbatches,
    arriving_microbatch,
    prenormal_scaling,
    attention_triple_matrix,
    exit_projection_matrix,
    mirrored_lookup_tile,
):
    layer_parameters = lax.all_gather(attention_triple_matrix[0], "seq", axis=0, tiled=True)
    compute_unit = lax.axis_index("seq")
    section_index = lax.axis_index("section")
    starting_result = transform_through_tier(
        resident_microbatches[0],
        prenormal_scaling[0],
        layer_parameters,
        exit_projection_matrix[0],
        mirrored_lookup_tile,
        compute_unit,
    )
    moved = from_behind(starting_result, "section", 1)
    second_in = jnp.where(section_index == 0, arriving_microbatch, moved)
    second_out = transform_through_tier(
        second_in,
        prenormal_scaling[0],
        layer_parameters,
        exit_projection_matrix[0],
        mirrored_lookup_tile,
        compute_unit,
    )
    return jnp.stack([starting_result, second_out])[:, None]


def solution(mesh):
    placed = (
        P("section", "seq", None),
        P("seq", None),
        P("section", None),
        P("section", "seq", None),
        P("section", None, None),
        P(),
    )
    return jax.shard_map(
        per_device,
        mesh=mesh,
        in_specs=placed,
        out_specs=P(None, "section", "seq", None),
        check_vma=False,
    )
```

profile of v0, /device:TPU:34, one launch (start us, length us, event | category | flops | bytes accessed | tf_op | source)
XLA Modules:
  0.0 360.5 jit_solution(13483647688169495418)
XLA Ops:
  6.5 0.7 all-gather.3.cloned.1.call-update
  7.3 1.1 fusion.54
  8.4 163.1 %all-gather.3.cloned.1.call-done = bf16[1,1024,3072]{2,1,0:T(8,128)(2,1)} async-done(((bf16[1,16,3072]{2,1,0:T(8,128)(2,1)}), bf16[1,1024,3072]{2,1,0:T(8,128)(2,1)}) %all-gather.3.cloned.1.call-update) | async-done | bytes 6291472 | tf_op jit(solution)/shard_map/all_gather | solution.py:84
  171.4 3.9 %fusion.2 = f32[128,3072]{1,0:T(8,128)S(1)} fusion(bf16[1,1024,3072]{2,1,0:T(8,128)(2,1)} %all-gather.3.cloned.1.call-done, bf16[1,128,1024]{2,1,0:T(8,128)(2,1)} %param.6, f32[1024]{0:T(1024)} %bitcast.157, f32[128]{0:T(128)S(1)} %add_rsqrt_fusion.5), kind=kOutput, calls=%fused_computation.2 | convolution fusion | flops 805830656 | bytes 8131072 | tf_op jit(solution)/shard_map/dot_general | solution.py:38
  175.4 1.1 copy-done.2
  177.3 2.4 multiply_bitcast_fusion.2
  179.7 0.9 pad_maximum_fusion.2
  180.6 3.5 collective-permute-start.2
  187.3 2.3 collective-permute-start.1
  189.6 1.9 collective-permute-start
  191.5 5.1 %collective-permute-start.3 = (bf16[2,128,1024]{2,1,0:T(8,128)(2,1)}, bf16[2,128,1024]{2,1,0:T(8,128)(2,1)}, u32[]{:S(2)}, u32[]{:S(2)}) collective-permute-start(bf16[2,128,1024]{2,1,0:T(8,128)(2,1)} %pad_maximum_fusion.2), channel_id=1, source_target_pairs={{0,8},{1,9},{2,10},{3,11},{4,12},{5,13},{6,14},{7,15},{8,0},{9,1},... | collective-permute-start | bytes 1572872 | tf_op jit(solution)/shard_map/ppermute | solution.py:14
  196.6 1.1 copy.82
  198.1 1.2 copy.83
  199.5 0.8 copy.61
  200.5 7.2 %collective-permute-done.2 = bf16[2,128,1024]{2,1,0:T(8,128)(2,1)} collective-permute-done((bf16[2,128,1024]{2,1,0:T(8,128)(2,1)}, bf16[2,128,1024]{2,1,0:T(8,128)(2,1)}, u32[]{:S(2)}, u32[]{:S(2)}) %collective-permute-start.2) | collective-permute-done | bytes 524320 | tf_op jit(solution)/shard_map/ppermute | solution.py:14
  207.7 1.0 constant_dynamic-slice_fusion.5
  208.6 12.4 %collective-permute-done.1 = bf16[2,128,1024]{2,1,0:T(8,128)(2,1)} collective-permute-done((bf16[2,128,1024]{2,1,0:T(8,128)(2,1)}, bf16[2,128,1024]{2,1,0:T(8,128)(2,1)}, u32[]{:S(2)}, u32[]{:S(2)}) %collective-permute-start.1) | collective-permute-done | bytes 524320 | tf_op jit(solution)/shard_map/ppermute | solution.py:14
  221.0 1.0 constant_dynamic-slice_fusion.6
  222.0 1.0 constant_dynamic-slice_fusion.7
  223.0 25.9 %collective-permute-done.3 = bf16[2,128,1024]{2,1,0:T(8,128)(2,1)} collective-permute-done((bf16[2,128,1024]{2,1,0:T(8,128)(2,1)}, bf16[2,128,1024]{2,1,0:T(8,128)(2,1)}, u32[]{:S(2)}, u32[]{:S(2)}) %collective-permute-start.3) | collective-permute-done | bytes 524320 | tf_op jit(solution)/shard_map/ppermute | solution.py:14
  248.9 1.0 constant_dynamic-slice_fusion.4
  250.6 1.8 multiply_exponential_fusion.1
  252.6 3.2 fusion.43
  255.8 1.1 copy.68
  257.4 3.5 collective-permute-start.4
  260.9 7.8 %collective-permute-done.4 = bf16[128,1024]{1,0:T(8,128)(2,1)S(1)} collective-permute-done((bf16[128,1024]{1,0:T(8,128)(2,1)S(1)}, bf16[128,1024]{1,0:T(8,128)(2,1)S(1)}, u32[]{:S(2)}, u32[]{:S(2)}) %collective-permute-start.4) | collective-permute-done | bytes 262176 | tf_op jit(solution)/shard_map/ppermute | solution.py:20
  268.9 3.8 %fusion = f32[128,3072]{1,0:T(8,128)S(1)} fusion(bf16[1,1024,3072]{2,1,0:T(8,128)(2,1)} %all-gather.3.cloned.1.call-done, bf16[128,1024]{1,0:T(8,128)(2,1)S(1)} %get-tuple-element.6, f32[128]{0:T(128)S(1)} %add_rsqrt_fusion.4, f32[1024]{0:T(1024)S(1)} %bitcast.158), kind=kOutput, calls=%fused_computation | convolution fusion | flops 805830656 | bytes 8131072 | tf_op jit(solution)/shard_map/dot_general | solution.py:38
  272.8 1.1 copy-done.1
  273.9 0.9 fusion.82
  275.5 2.2 multiply_bitcast_fusion
  277.8 0.8 pad_maximum_fusion.3
  278.6 1.9 collective-permute-start.7
  280.5 2.0 collective-permute-start.6
  282.5 1.9 collective-permute-start.5
  284.9 8.3 %collective-permute-start.8 = (bf16[2,128,1024]{2,1,0:T(8,128)(2,1)}, bf16[2,128,1024]{2,1,0:T(8,128)(2,1)}, u32[]{:S(2)}, u32[]{:S(2)}) collective-permute-start(bf16[2,128,1024]{2,1,0:T(8,128)(2,1)} %pad_maximum_fusion.3), channel_id=1, source_target_pairs={{0,8},{1,9},{2,10},{3,11},{4,12},{5,13},{6,14},{7,15},{8,0},{9,1},... | collective-permute-start | bytes 1572872 | tf_op jit(solution)/shard_map/ppermute | solution.py:14
  293.2 1.1 copy.92
  294.6 1.0 copy.96
  295.6 0.8 copy.72
  296.5 8.6 %collective-permute-done.7 = bf16[2,128,1024]{2,1,0:T(8,128)(2,1)} collective-permute-done((bf16[2,128,1024]{2,1,0:T(8,128)(2,1)}, bf16[2,128,1024]{2,1,0:T(8,128)(2,1)}, u32[]{:S(2)}, u32[]{:S(2)}) %collective-permute-start.7) | collective-permute-done | bytes 524320 | tf_op jit(solution)/shard_map/ppermute | solution.py:14
  305.1 1.0 constant_dynamic-slice_fusion.1
  306.1 1.0 constant_dynamic-slice_fusion.2
  307.1 1.0 constant_dynamic-slice_fusion.3
  308.0 35.8 %collective-permute-done.8 = bf16[2,128,1024]{2,1,0:T(8,128)(2,1)} collective-permute-done((bf16[2,128,1024]{2,1,0:T(8,128)(2,1)}, bf16[2,128,1024]{2,1,0:T(8,128)(2,1)}, u32[]{:S(2)}, u32[]{:S(2)}) %collective-permute-start.8) | collective-permute-done | bytes 524320 | tf_op jit(solution)/shard_map/ppermute | solution.py:14
  343.9 1.0 constant_dynamic-slice_fusion
  345.6 1.8 multiply_exponential_fusion
  347.6 3.2 fusion.46
  350.7 1.1 copy.79
  352.8 0.8 maximum_bitcast_fusion
  (79 shorter events, 7.1 us)
Async XLA Ops:
  6.5 250.4 %copy-start = (bf16[1,1024,1024]{2,1,0:T(8,128)(2,1)S(1)}, bf16[1,1024,1024]{2,1,0:T(8,128)(2,1)}, u32[]{:S(2)}) copy-start(bf16[1,1024,1024]{2,1,0:T(8,128)(2,1)} %param.10) | copy-start | bytes 6291460
  6.5 164.9 %all-gather.3.cloned.1.call-start = ((), (), s32[]{:S(2)}) async-start(), calls=%async_computation | async-start | bytes 6389760 | tf_op jit(solution)/shard_map/all_gather | solution.py:84
  175.4 1.1 copy-start.2
  177.3 6.8 %copy-start.9 = (s32[64,4]{0,1:T(4,128)S(1)}, s32[64,4]{0,1:T(4,128)}, u32[]{:S(2)}) copy-start(s32[64,4]{0,1:T(4,128)} %param.11) | copy-start | bytes 3076
  180.6 27.1 %collective-permute-start.2 = (bf16[2,128,1024]{2,1,0:T(8,128)(2,1)}, bf16[2,128,1024]{2,1,0:T(8,128)(2,1)}, u32[]{:S(2)}, u32[]{:S(2)}) collective-permute-start(bf16[2,128,1024]{2,1,0:T(8,128)(2,1)} %pad_maximum_fusion.2), channel_id=1, source_target_pairs={{0,4},{1,5},{2,6},{3,7},{4,0},{5,1},{6,2},{7,3},{8,12},{9,13},{10,... | collective-permute-start | bytes 1572872 | tf_op jit(solution)/shard_map/ppermute | solution.py:14
  187.3 33.8 %collective-permute-start.1 = (bf16[2,128,1024]{2,1,0:T(8,128)(2,1)}, bf16[2,128,1024]{2,1,0:T(8,128)(2,1)}, u32[]{:S(2)}, u32[]{:S(2)}) collective-permute-start(bf16[2,128,1024]{2,1,0:T(8,128)(2,1)} %pad_maximum_fusion.2), channel_id=1, source_target_pairs={{0,2},{1,3},{2,0},{3,1},{4,6},{5,7},{6,4},{7,5},{8,10},{9,11},{10,... | collective-permute-start | bytes 1572872 | tf_op jit(solution)/shard_map/ppermute | solution.py:14
  189.6 32.4 %collective-permute-start = (bf16[2,128,1024]{2,1,0:T(8,128)(2,1)}, bf16[2,128,1024]{2,1,0:T(8,128)(2,1)}, u32[]{:S(2)}, u32[]{:S(2)}) collective-permute-start(bf16[2,128,1024]{2,1,0:T(8,128)(2,1)} %pad_maximum_fusion.2), channel_id=1, source_target_pairs={{0,1},{1,0},{2,3},{3,2},{4,5},{5,4},{6,7},{7,6},{8,9},{9,8},{10,11... | collective-permute-start | bytes 1572872 | tf_op jit(solution)/shard_map/ppermute | solution.py:14
  191.5 57.4 %collective-permute-start.3 = (bf16[2,128,1024]{2,1,0:T(8,128)(2,1)}, bf16[2,128,1024]{2,1,0:T(8,128)(2,1)}, u32[]{:S(2)}, u32[]{:S(2)}) collective-permute-start(bf16[2,128,1024]{2,1,0:T(8,128)(2,1)} %pad_maximum_fusion.2), channel_id=1, source_target_pairs={{0,8},{1,9},{2,10},{3,11},{4,12},{5,13},{6,14},{7,15},{8,0},{9,1},... | collective-permute-start | bytes 1572872 | tf_op jit(solution)/shard_map/ppermute | solution.py:14
  252.6 4.4 %copy-start.3 = (bf16[1,128,1024]{2,1,0:T(8,128)(2,1)S(1)}, bf16[1,128,1024]{2,1,0:T(8,128)(2,1)}, u32[]{:S(2)}) copy-start(bf16[1,128,1024]{2,1,0:T(8,128)(2,1)} %param.6) | copy-start | bytes 786436
  256.9 11.8 %copy-start.7 = (bf16[128,1024]{1,0:T(8,128)(2,1)S(1)}, bf16[128,1024]{1,0:T(8,128)(2,1)}, u32[]{:S(2)}) copy-start(bf16[128,1024]{1,0:T(8,128)(2,1)} %param.7) | copy-start | bytes 786436
  256.9 12.0 %copy-start.8 = (f32[1,1024]{1,0:T(1,128)S(1)}, f32[1,1024]{1,0:T(1,128)}, u32[]{:S(2)}) copy-start(f32[1,1024]{1,0:T(1,128)} %param.8) | copy-start | bytes 12292
  257.4 15.4 %copy-start.5 = (bf16[128,1024]{1,0:T(8,128)(2,1)}, bf16[128,1024]{1,0:T(8,128)(2,1)S(1)}, u32[]{:S(2)}) copy-start(bf16[128,1024]{1,0:T(8,128)(2,1)S(1)} %fusion.37) | copy-start | bytes 786436
  257.4 11.3 %collective-permute-start.4 = (bf16[128,1024]{1,0:T(8,128)(2,1)S(1)}, bf16[128,1024]{1,0:T(8,128)(2,1)S(1)}, u32[]{:S(2)}, u32[]{:S(2)}) collective-permute-start(bf16[128,1024]{1,0:T(8,128)(2,1)S(1)} %fusion.37), channel_id=1, source_target_pairs={{0,64},{64,128},{128,192},{192,256},{256,320},{320,384},{384,448},... | collective-permute-start | bytes 786440 | tf_op jit(solution)/shard_map/ppermute | solution.py:20
  272.8 1.2 copy-start.1
  275.5 2.3 copy-start.4
  278.6 26.5 %collective-permute-start.7 = (bf16[2,128,1024]{2,1,0:T(8,128)(2,1)}, bf16[2,128,1024]{2,1,0:T(8,128)(2,1)}, u32[]{:S(2)}, u32[]{:S(2)}) collective-permute-start(bf16[2,128,1024]{2,1,0:T(8,128)(2,1)} %pad_maximum_fusion.3), channel_id=1, source_target_pairs={{0,4},{1,5},{2,6},{3,7},{4,0},{5,1},{6,2},{7,3},{8,12},{9,13},{10,... | collective-permute-start | bytes 1572872 | tf_op jit(solution)/shard_map/ppermute | solution.py:14
  280.5 25.5 %collective-permute-start.6 = (bf16[2,128,1024]{2,1,0:T(8,128)(2,1)}, bf16[2,128,1024]{2,1,0:T(8,128)(2,1)}, u32[]{:S(2)}, u32[]{:S(2)}) collective-permute-start(bf16[2,128,1024]{2,1,0:T(8,128)(2,1)} %pad_maximum_fusion.3), channel_id=1, source_target_pairs={{0,2},{1,3},{2,0},{3,1},{4,6},{5,7},{6,4},{7,5},{8,10},{9,11},{10,... | collective-permute-start | bytes 1572872 | tf_op jit(solution)/shard_map/ppermute | solution.py:14
  282.5 24.5 %collective-permute-start.5 = (bf16[2,128,1024]{2,1,0:T(8,128)(2,1)}, bf16[2,128,1024]{2,1,0:T(8,128)(2,1)}, u32[]{:S(2)}, u32[]{:S(2)}) collective-permute-start(bf16[2,128,1024]{2,1,0:T(8,128)(2,1)} %pad_maximum_fusion.3), channel_id=1, source_target_pairs={{0,1},{1,0},{2,3},{3,2},{4,5},{5,4},{6,7},{7,6},{8,9},{9,8},{10,11... | collective-permute-start | bytes 1572872 | tf_op jit(solution)/shard_map/ppermute | solution.py:14
  284.9 59.0 %collective-permute-start.8 = (bf16[2,128,1024]{2,1,0:T(8,128)(2,1)}, bf16[2,128,1024]{2,1,0:T(8,128)(2,1)}, u32[]{:S(2)}, u32[]{:S(2)}) collective-permute-start(bf16[2,128,1024]{2,1,0:T(8,128)(2,1)} %pad_maximum_fusion.3), channel_id=1, source_target_pairs={{0,8},{1,9},{2,10},{3,11},{4,12},{5,13},{6,14},{7,15},{8,0},{9,1},... | collective-permute-start | bytes 1572872 | tf_op jit(solution)/shard_map/ppermute | solution.py:14
  351.9 1.0 copy-start.6
Sparse Core Ops, SparseCore 0:
  10.6 160.7 all-gather.2
where the time goes:
time: 362 us; the launch traced here: 360 us
  waiting for transfers between devices  261 us (72%)
  starting transfers between devices  30.4 us (8%)
  local copies, waits for them, and re-layouts  23.6 us (7%)
  matrix products  18.6 us (5%)
  between operations  16.4 us (5%)
  other arithmetic  9.93 us (3%)
    all_gather x1, waiting for transfers between devices, per_device(): lax.all_gather(attention_triple_matrix[0], 'seq', axis=0, tiled=True)  163 us
    ppermute x8, waiting for transfers between devices, swapped(): lax.ppermute(x, axis, [(i, i ^ 1 << stride) for i in range(lax.axis_size(...  89.9 us
    ppermute x8, starting transfers between devices, swapped(): lax.ppermute(x, axis, [(i, i ^ 1 << stride) for i in range(lax.axis_size(...  27 us
    unnamed x38, local copies, waits for them, and re-layouts  9.15 us
    ppermute x1, waiting for transfers between devices, from_behind(): return lax.ppermute(block, axis, route)  7.83 us
    dynamic_slice x8, local copies, waits for them, and re-layouts, transform_through_tier(): remote.append(lax.dynamic_slice_in_dim(arrived, wanted * BLOCK, BLOCK, 1))  7.78 us
    dot_general x2, matrix products, transform_through_tier(): projected = jnp.dot(normed, weights, preferred_element_type=jnp.float32)  7.77 us
  transfers between devices with their start and end apart: 10, of which 7 were waited for; matrix products, arithmetic and copies ran while one was open for 4% of the time, Pallas kernels for 0%

commit v1 on v0

--- a/solution.py
+++ b/solution.py
@@ -8,6 +8,13 @@
 BLOCK = 64
 LEVELS = 4
 epsilon = 1e-06
+
+
+def gather_over(x, axis, along):
+    devices = lax.axis_size(axis)
+    blocks = jnp.stack([x for _ in range(devices)])
+    blocks = lax.all_to_all(blocks, axis, split_axis=0, concat_axis=0)
+    return jnp.concatenate(blocks, axis=along)
 
 
 def swapped(x, axis, stride):
@@ -81,7 +88,7 @@
     exit_projection_matrix,
     mirrored_lookup_tile,
 ):
-    layer_parameters = lax.all_gather(attention_triple_matrix[0], "seq", axis=0, tiled=True)
+    layer_parameters = gather_over(attention_triple_matrix[0], "seq", 0)
     compute_unit = lax.axis_index("seq")
     section_index = lax.axis_index("section")
     starting_result = transform_through_tier(

time: 362 us -> 482 us (1.33)
  the two profiles are of different devices: /device:TPU:34 before, /device:TPU:167 now
where the time goes in v1:
time: 482 us; the launch traced here: 481 us
  waiting for transfers between devices  363 us (75%)
  starting transfers between devices  57.6 us (12%)
  local copies, waits for them, and re-layouts  30 us (6%)
  matrix products  18.6 us (4%)
  other arithmetic  8.98 us (2%)
    all_to_all x1, waiting for transfers between devices, gather_over(): blocks = lax.all_to_all(blocks, axis, split_axis=0, concat_axis=0)  274 us
    ppermute x8, waiting for transfers between devices, swapped(): lax.ppermute(x, axis, [(i, i ^ 1 << stride) for i in range(lax.axis_size(...  82.8 us
    ppermute x8, starting transfers between devices, swapped(): lax.ppermute(x, axis, [(i, i ^ 1 << stride) for i in range(lax.axis_size(...  37.3 us
    all_to_all x1, starting transfers between devices, gather_over(): blocks = lax.all_to_all(blocks, axis, split_axis=0, concat_axis=0)  17.1 us
    unnamed x40, local copies, waits for them, and re-layouts  11.1 us
  transfers between devices with their start and end apart: 10, of which 6 were waited for; matrix products, arithmetic and copies ran while one was open for 3% of the time, Pallas kernels for 0%

profile of v1, /device:TPU:167, one launch (start us, length us, event | category | flops | bytes accessed | tf_op | source)
XLA Modules:
  0.0 481.3 jit_solution(403139046214456172)
XLA Ops:
  0.0 4.5 stack.24
  4.5 17.1 %all-to-all-start = ((bf16[64,16,3072]{2,1,0:T(8,128)(2,1)}), bf16[64,16,3072]{2,1,0:T(8,128)(2,1)}, u32[]{:S(2)}, u32[]{:S(2)}) async-start(bf16[64,16,3072]{2,1,0:T(8,128)(2,1)} %stack.24), calls=%async_computation | async-start | bytes 12582912 | tf_op jit(solution)/shard_map/all_to_all | solution.py:16
  21.7 274.3 %all-to-all-done = bf16[64,16,3072]{2,1,0:T(8,128)(2,1)} async-done(((bf16[64,16,3072]{2,1,0:T(8,128)(2,1)}), bf16[64,16,3072]{2,1,0:T(8,128)(2,1)}, u32[]{:S(2)}, u32[]{:S(2)}) %all-to-all-start) | async-done | bytes 6291488 | tf_op jit(solution)/shard_map/all_to_all | solution.py:16
  296.1 3.8 fusion.67
  299.9 0.9 fusion.79
  301.9 2.4 multiply_bitcast_fusion.2
  304.3 0.9 pad_maximum_fusion.2
  305.2 2.5 collective-permute-start.3
  310.9 1.9 collective-permute-start.2
  312.8 3.1 collective-permute-start.1
  315.9 5.4 %collective-permute-start = (bf16[2,128,1024]{2,1,0:T(8,128)(2,1)}, bf16[2,128,1024]{2,1,0:T(8,128)(2,1)}, u32[]{:S(2)}, u32[]{:S(2)}) collective-permute-start(bf16[2,128,1024]{2,1,0:T(8,128)(2,1)} %pad_maximum_fusion.2), channel_id=1, source_target_pairs={{0,1},{1,0},{2,3},{3,2},{4,5},{5,4},{6,7},{7,6},{8,9},{9,8},{10,11... | collective-permute-start | bytes 1572872 | tf_op jit(solution)/shard_map/ppermute | solution.py:21
  321.3 1.1 copy.82
  322.8 1.0 copy.87
  324.6 1.1 copy.83
  325.7 0.9 copy.81
  326.9 20.2 %collective-permute-done.3 = bf16[2,128,1024]{2,1,0:T(8,128)(2,1)} collective-permute-done((bf16[2,128,1024]{2,1,0:T(8,128)(2,1)}, bf16[2,128,1024]{2,1,0:T(8,128)(2,1)}, u32[]{:S(2)}, u32[]{:S(2)}) %collective-permute-start.3) | collective-permute-done | bytes 524320 | tf_op jit(solution)/shard_map/ppermute | solution.py:21
  347.1 1.0 constant_dynamic-slice_fusion.4
  348.1 1.0 constant_dynamic-slice_fusion.5
  349.1 17.5 %collective-permute-done.1 = bf16[2,128,1024]{2,1,0:T(8,128)(2,1)} collective-permute-done((bf16[2,128,1024]{2,1,0:T(8,128)(2,1)}, bf16[2,128,1024]{2,1,0:T(8,128)(2,1)}, u32[]{:S(2)}, u32[]{:S(2)}) %collective-permute-start.1) | collective-permute-done | bytes 524320 | tf_op jit(solution)/shard_map/ppermute | solution.py:21
  366.6 1.0 constant_dynamic-slice_fusion.6
  367.6 1.0 constant_dynamic-slice_fusion.7
  369.3 0.8 copy-done.4
  370.0 1.8 multiply_exponential_fusion.1
  372.0 3.2 fusion.39
  375.2 1.1 copy.68
  376.8 3.2 collective-permute-start.4
  380.0 6.0 %collective-permute-done.4 = bf16[128,1024]{1,0:T(8,128)(2,1)S(1)} collective-permute-done((bf16[128,1024]{1,0:T(8,128)(2,1)S(1)}, bf16[128,1024]{1,0:T(8,128)(2,1)S(1)}, u32[]{:S(2)}, u32[]{:S(2)}) %collective-permute-start.4) | collective-permute-done | bytes 262176 | tf_op jit(solution)/shard_map/ppermute | solution.py:27
  386.3 3.8 fusion.64
  390.1 1.0 fusion.81
  392.2 2.2 multiply_bitcast_fusion
  394.5 0.8 pad_maximum_fusion.3
  395.3 4.5 collective-permute-start.8
  399.8 11.5 %collective-permute-start.7 = (bf16[2,128,1024]{2,1,0:T(8,128)(2,1)}, bf16[2,128,1024]{2,1,0:T(8,128)(2,1)}, u32[]{:S(2)}, u32[]{:S(2)}) collective-permute-start(bf16[2,128,1024]{2,1,0:T(8,128)(2,1)} %pad_maximum_fusion.3), channel_id=1, source_target_pairs={{0,4},{1,5},{2,6},{3,7},{4,0},{5,1},{6,2},{7,3},{8,12},{9,13},{10,... | collective-permute-start | bytes 1572872 | tf_op jit(solution)/shard_map/ppermute | solution.py:21
  411.3 4.1 collective-permute-start.6
  415.4 4.2 collective-permute-start.5
  420.1 1.0 copy.96
  421.2 0.8 copy.72
  422.0 1.1 copy.90
  423.5 13.4 %collective-permute-done.8 = bf16[2,128,1024]{2,1,0:T(8,128)(2,1)} collective-permute-done((bf16[2,128,1024]{2,1,0:T(8,128)(2,1)}, bf16[2,128,1024]{2,1,0:T(8,128)(2,1)}, u32[]{:S(2)}, u32[]{:S(2)}) %collective-permute-start.8) | collective-permute-done | bytes 524320 | tf_op jit(solution)/shard_map/ppermute | solution.py:21
  436.8 1.0 constant_dynamic-slice_fusion
  437.8 1.0 constant_dynamic-slice_fusion.1
  438.8 31.7 %collective-permute-done.6 = bf16[2,128,1024]{2,1,0:T(8,128)(2,1)} collective-permute-done((bf16[2,128,1024]{2,1,0:T(8,128)(2,1)}, bf16[2,128,1024]{2,1,0:T(8,128)(2,1)}, u32[]{:S(2)}, u32[]{:S(2)}) %collective-permute-start.6) | collective-permute-done | bytes 524320 | tf_op jit(solution)/shard_map/ppermute | solution.py:21
  470.5 1.0 constant_dynamic-slice_fusion.2
  471.5 1.0 constant_dynamic-slice_fusion.3
  473.2 1.8 multiply_exponential_fusion
  475.1 3.2 fusion.42
  478.4 1.1 copy.79
  480.5 0.8 maximum_bitcast_fusion
  (81 shorter events, 8.4 us)
Async XLA Ops:
  0.0 376.4 %copy-start = (bf16[1,1024,1024]{2,1,0:T(8,128)(2,1)S(1)}, bf16[1,1024,1024]{2,1,0:T(8,128)(2,1)}, u32[]{:S(2)}) copy-start(bf16[1,1024,1024]{2,1,0:T(8,128)(2,1)} %param.10) | copy-start | bytes 6291460
  4.5 17.1 %copy-start.3 = (bf16[1,128,1024]{2,1,0:T(8,128)(2,1)S(1)}, bf16[1,128,1024]{2,1,0:T(8,128)(2,1)}, u32[]{:S(2)}) copy-start(bf16[1,128,1024]{2,1,0:T(8,128)(2,1)} %param.6) | copy-start | bytes 786436
  4.5 291.6 %copy-start.9 = (f32[1,1024]{1,0:T(1,128)S(1)}, f32[1,1024]{1,0:T(1,128)}, u32[]{:S(2)}) copy-start(f32[1,1024]{1,0:T(1,128)} %param.8) | copy-start | bytes 12292
  4.5 291.6 %all-to-all-start = ((bf16[64,16,3072]{2,1,0:T(8,128)(2,1)}), bf16[64,16,3072]{2,1,0:T(8,128)(2,1)}, u32[]{:S(2)}, u32[]{:S(2)}) async-start(bf16[64,16,3072]{2,1,0:T(8,128)(2,1)} %stack.24), calls=%async_computation | async-start | bytes 12582912 | tf_op jit(solution)/shard_map/all_to_all | solution.py:16
  299.9 1.2 copy-start.2
  301.9 5.8 %copy-start.10 = (s32[64,4]{0,1:T(4,128)S(1)}, s32[64,4]{0,1:T(4,128)}, u32[]{:S(2)}) copy-start(s32[64,4]{0,1:T(4,128)} %param.11) | copy-start | bytes 3076
  305.2 41.9 %collective-permute-start.3 = (bf16[2,128,1024]{2,1,0:T(8,128)(2,1)}, bf16[2,128,1024]{2,1,0:T(8,128)(2,1)}, u32[]{:S(2)}, u32[]{:S(2)}) collective-permute-start(bf16[2,128,1024]{2,1,0:T(8,128)(2,1)} %pad_maximum_fusion.2), channel_id=1, source_target_pairs={{0,8},{1,9},{2,10},{3,11},{4,12},{5,13},{6,14},{7,15},{8,0},{9,1},... | collective-permute-start | bytes 1572872 | tf_op jit(solution)/shard_map/ppermute | solution.py:21
  310.9 37.2 %collective-permute-start.2 = (bf16[2,128,1024]{2,1,0:T(8,128)(2,1)}, bf16[2,128,1024]{2,1,0:T(8,128)(2,1)}, u32[]{:S(2)}, u32[]{:S(2)}) collective-permute-start(bf16[2,128,1024]{2,1,0:T(8,128)(2,1)} %pad_maximum_fusion.2), channel_id=1, source_target_pairs={{0,4},{1,5},{2,6},{3,7},{4,0},{5,1},{6,2},{7,3},{8,12},{9,13},{10,... | collective-permute-start | bytes 1572872 | tf_op jit(solution)/shard_map/ppermute | solution.py:21
  312.8 53.8 %collective-permute-start.1 = (bf16[2,128,1024]{2,1,0:T(8,128)(2,1)}, bf16[2,128,1024]{2,1,0:T(8,128)(2,1)}, u32[]{:S(2)}, u32[]{:S(2)}) collective-permute-start(bf16[2,128,1024]{2,1,0:T(8,128)(2,1)} %pad_maximum_fusion.2), channel_id=1, source_target_pairs={{0,2},{1,3},{2,0},{3,1},{4,6},{5,7},{6,4},{7,5},{8,10},{9,11},{10,... | collective-permute-start | bytes 1572872 | tf_op jit(solution)/shard_map/ppermute | solution.py:21
  315.9 51.7 %collective-permute-start = (bf16[2,128,1024]{2,1,0:T(8,128)(2,1)}, bf16[2,128,1024]{2,1,0:T(8,128)(2,1)}, u32[]{:S(2)}, u32[]{:S(2)}) collective-permute-start(bf16[2,128,1024]{2,1,0:T(8,128)(2,1)} %pad_maximum_fusion.2), channel_id=1, source_target_pairs={{0,1},{1,0},{2,3},{3,2},{4,5},{5,4},{6,7},{7,6},{8,9},{9,8},{10,11... | collective-permute-start | bytes 1572872 | tf_op jit(solution)/shard_map/ppermute | solution.py:21
  369.0 1.0 copy-start.4
  376.4 9.7 %copy-start.8 = (bf16[128,1024]{1,0:T(8,128)(2,1)S(1)}, bf16[128,1024]{1,0:T(8,128)(2,1)}, u32[]{:S(2)}) copy-start(bf16[128,1024]{1,0:T(8,128)(2,1)} %param.7) | copy-start | bytes 786436
  376.8 13.3 %copy-start.6 = (bf16[128,1024]{1,0:T(8,128)(2,1)}, bf16[128,1024]{1,0:T(8,128)(2,1)S(1)}, u32[]{:S(2)}) copy-start(bf16[128,1024]{1,0:T(8,128)(2,1)S(1)} %fusion.33) | copy-start | bytes 786436
  376.8 9.2 %collective-permute-start.4 = (bf16[128,1024]{1,0:T(8,128)(2,1)S(1)}, bf16[128,1024]{1,0:T(8,128)(2,1)S(1)}, u32[]{:S(2)}, u32[]{:S(2)}) collective-permute-start(bf16[128,1024]{1,0:T(8,128)(2,1)S(1)} %fusion.33), channel_id=1, source_target_pairs={{0,64},{64,128},{128,192},{192,256},{256,320},{320,384},{384,448},... | collective-permute-start | bytes 786440 | tf_op jit(solution)/shard_map/ppermute | solution.py:27
  390.1 1.4 copy-start.1
  392.2 2.3 copy-start.5
  395.3 41.5 %collective-permute-start.8 = (bf16[2,128,1024]{2,1,0:T(8,128)(2,1)}, bf16[2,128,1024]{2,1,0:T(8,128)(2,1)}, u32[]{:S(2)}, u32[]{:S(2)}) collective-permute-start(bf16[2,128,1024]{2,1,0:T(8,128)(2,1)} %pad_maximum_fusion.3), channel_id=1, source_target_pairs={{0,8},{1,9},{2,10},{3,11},{4,12},{5,13},{6,14},{7,15},{8,0},{9,1},... | collective-permute-start | bytes 1572872 | tf_op jit(solution)/shard_map/ppermute | solution.py:21
  399.8 38.0 %collective-permute-start.7 = (bf16[2,128,1024]{2,1,0:T(8,128)(2,1)}, bf16[2,128,1024]{2,1,0:T(8,128)(2,1)}, u32[]{:S(2)}, u32[]{:S(2)}) collective-permute-start(bf16[2,128,1024]{2,1,0:T(8,128)(2,1)} %pad_maximum_fusion.3), channel_id=1, source_target_pairs={{0,4},{1,5},{2,6},{3,7},{4,0},{5,1},{6,2},{7,3},{8,12},{9,13},{10,... | collective-permute-start | bytes 1572872 | tf_op jit(solution)/shard_map/ppermute | solution.py:21
  411.3 59.2 %collective-permute-start.6 = (bf16[2,128,1024]{2,1,0:T(8,128)(2,1)}, bf16[2,128,1024]{2,1,0:T(8,128)(2,1)}, u32[]{:S(2)}, u32[]{:S(2)}) collective-permute-start(bf16[2,128,1024]{2,1,0:T(8,128)(2,1)} %pad_maximum_fusion.3), channel_id=1, source_target_pairs={{0,2},{1,3},{2,0},{3,1},{4,6},{5,7},{6,4},{7,5},{8,10},{9,11},{10,... | collective-permute-start | bytes 1572872 | tf_op jit(solution)/shard_map/ppermute | solution.py:21
  415.4 56.0 %collective-permute-start.5 = (bf16[2,128,1024]{2,1,0:T(8,128)(2,1)}, bf16[2,128,1024]{2,1,0:T(8,128)(2,1)}, u32[]{:S(2)}, u32[]{:S(2)}) collective-permute-start(bf16[2,128,1024]{2,1,0:T(8,128)(2,1)} %pad_maximum_fusion.3), channel_id=1, source_target_pairs={{0,1},{1,0},{2,3},{3,2},{4,5},{5,4},{6,7},{7,6},{8,9},{9,8},{10,11... | collective-permute-start | bytes 1572872 | tf_op jit(solution)/shard_map/ppermute | solution.py:21
  479.5 1.0 copy-start.7
